TPU v7x, 32 devices: a whole 2x2x4 slice. The times are simulated.
32 devices in a mesh: space: 4 (over x, core), tm: 8 (over z, y).
Axes of the slice: x: 2, y: 2, z: 4, core: 2. Of those that a mesh axis runs over, the one named last changes fastest.
Arguments:
- snapshots: bfloat16 [4096, 65536], P('tm', 'space'), may hold values from -24 to 24
- freq_bins: int32 [2], replicated, may hold values from 1 to 127
Outputs:
- gram_matrix: float32 [2, 64, 64], replicated
- whitened: float32 [2, 64, 65536], P(None, None, ('space', 'tm'))
All inputs are finite; a program needn't handle non-finite values.
Results may differ from a plain program's by a relative error of at most 0.0041.
Values may be sent and summed in bfloat16 or wider, within the bound.
No kernel may reach another device: no remote copies, remote signals or barrier semaphores. Data moves between devices by JAX's collectives and lax.ppermute only.
A program may use at most 128 MiB of HBM per device.

v0:
```python
import jax
import jax.numpy as jnp
from jax import lax
from jax.sharding import PartitionSpec as P

NFFT = 256
HOP = 128
NF = 2
ridge_term = 0.01


def passed_along(array, axis, by):
    devices = lax.axis_size(axis)
    return lax.ppermute(array, axis, [(i, (i + by) % devices) for i in range(devices)])


def make_table(freq_bins):
    sample = jnp.arange(NFFT, dtype=jnp.int32)
    sample_f = sample.astype(jnp.float32)
    hann_taper = 0.5 - 0.5 * jnp.cos(2.0 * jnp.pi * sample_f / NFFT)
    window = hann_taper / jnp.sqrt(jnp.sum(hann_taper * hann_taper))
    phase_idx = freq_bins[:, None] * sample[None, :] % NFFT
    angles = 2.0 * jnp.pi * phase_idx.astype(jnp.float32) / NFFT
    table = jnp.stack([window * jnp.cos(angles), -window * jnp.sin(angles)], axis=1)
    return table.astype(jnp.bfloat16)


def on_device(snapshots, freq_bins):
    points = snapshots.shape[1]
    block_count = snapshots.shape[0] // HOP
    table_rows = make_table(freq_bins).reshape(NF * 2, NFFT)
    first_table = table_rows[:, :HOP]
    second_table = table_rows[:, HOP:]
    halves = snapshots.reshape(block_count, HOP, points)
    lead_part = jnp.einsum("ct,htp->chp", first_table, halves, preferred_element_type=jnp.float32)
    trail_part = jnp.einsum("ct,htp->chp", second_table, halves, preferred_element_type=jnp.float32)
    incoming = passed_along(trail_part[:, :1], "tm", -1)
    trail_own = trail_part[:, 1:]
    coeffs = lead_part + jnp.concatenate([trail_own, incoming], axis=1)
    slice_width = points // lax.axis_size("tm")
    position = lax.axis_index("tm") * slice_width
    local_cols = lax.dynamic_slice_in_dim(
        lax.all_gather(coeffs, "tm", axis=1, tiled=True), position, slice_width, 2
    )
    all_blocks_count = local_cols.shape[1]
    columns = local_cols.reshape(NF, 2 * all_blocks_count, slice_width)
    grid_total = points * lax.axis_size("space")
    partial_value = (
        jnp.einsum("fcp,fdp->fcd", columns, columns, precision=lax.Precision.HIGHEST) / grid_total
    )
    gram_matrix = lax.psum(partial_value, ("space", "tm"))
    identity = jnp.eye(2 * all_blocks_count, dtype=jnp.float32)
    factor = jnp.linalg.cholesky(gram_matrix + ridge_term * identity[None])
    whitened = lax.linalg.triangular_solve(factor, columns, left_side=True, lower=True)
    return (gram_matrix, whitened)


def solution(mesh):
    placed = (P("tm", "space"), P())
    return jax.shard_map(
        on_device,
        mesh=mesh,
        in_specs=placed,
        out_specs=(P(), P(None, None, ("space", "tm"))),
        check_vma=False,
    )
```

profile of v0, /device:TPU:0, one launch (start us, length us, event | category | flops | bytes accessed | tf_op | source)
XLA Modules:
  0.0 232.3 jit_solution(7412217076847700622)
XLA Ops:
  7.2 0.0 all-gather.2.cloned.1.call-start
  7.2 0.6 multiply_reduce_fusion
  8.6 0.8 multiply_convert_fusion.1
  9.4 0.0 copy-start
  9.4 8.2 %fusion.6 = f32[4,4,16384]{2,0,1:T(4,128)S(1)} fusion(bf16[4,128,16384]{2,1,0:T(8,128)(2,1)} %bitcast.24, bf16[4,256]{1,0:T(4,128)(2,1)S(1)} %convert_element_type.35), kind=kOutput, calls=%fused_computation.23 | convolution fusion | flops 67108864 | bytes 17826816 | tf_op jit(solution)/shard_map/ct,htp->chp/dot_general | solution.py:36
  17.7 6.1 %collective-permute-start = (f32[4,1,16384]{2,0,1:T(4,128)S(1)}, f32[4,1,16384]{2,0,1:T(4,128)S(1)}, u32[]{:S(2)}, u32[]{:S(2)}) collective-permute-start(f32[4,1,16384]{2,0,1:T(4,128)S(1)} %slice.29), channel_id=1, source_target_pairs={{0,7},{1,0},{2,1},{3,2},{4,3},{5,4},{6,5},{7,6},{8,15},{9,8},{10,9... | collective-permute-start | bytes 786440 | tf_op jit(solution)/shard_map/ppermute | solution.py:14
  23.7 0.1 slice.28
  23.8 5.5 %collective-permute-done = f32[4,1,16384]{2,0,1:T(4,128)S(1)} collective-permute-done((f32[4,1,16384]{2,0,1:T(4,128)S(1)}, f32[4,1,16384]{2,0,1:T(4,128)S(1)}, u32[]{:S(2)}, u32[]{:S(2)}) %collective-permute-start) | collective-permute-done | bytes 262176 | tf_op jit(solution)/shard_map/ppermute | solution.py:14
  29.3 0.0 copy-done
  29.3 3.3 %maximum_add_fusion = f32[4,4,16384]{2,0,1:T(4,128)} fusion(f32[4,1,16384]{2,0,1:T(4,128)S(1)} %collective-permute-done, f32[4,3,16384]{2,0,1:T(4,128)S(1)} %slice.28, bf16[4,128,16384]{2,1,0:T(8,128)(2,1)S(1)} %bitcast.25, bf16[4,256]{1,0:T(4,128)(2,1)S(1)} %convert_element_type.35), kind=kOutput, calls=%fused_computation.1 | convolution fusion | flops 67633152 | bytes 18875392 | tf_op jit(solution)/shard_map/ct,htp->chp/dot_general | solution.py:35
  32.6 0.0 all-gather.2.cloned.1.call-update
  32.6 0.1 copy.36
  32.7 126.4 %all-gather.2.cloned.1.call-done = f32[4,32,16384]{2,0,1:T(4,128)} async-done(((f32[4,4,16384]{2,0,1:T(4,128)}), f32[4,32,16384]{2,0,1:T(4,128)}) %all-gather.2.cloned.1.call-update) | async-done | bytes 8388624 | tf_op jit(solution)/shard_map/all_gather | solution.py:43
  159.1 1.3 constant_dynamic-slice_fusion
  160.4 0.6 copy.42
  161.0 1.1 convolution_multiply_fusion
  162.1 38.7 %psum.7 = f32[2,64,64]{1,2,0:T(8,128)S(1)} all-reduce(f32[2,64,64]{1,2,0:T(8,128)S(1)} %convolution_multiply_fusion), channel_id=1, replica_groups=mesh['space'=4,'tm'=8] {'space','tm'}, use_global_device_ids=true, to_apply=%region_1.2 | all-reduce | flops 8192 | bytes 65536 | tf_op jit(solution)/shard_map/psum | solution.py:51
  200.8 0.7 copy.39
  201.5 0.1 copy.37
  201.6 11.7 %custom-call.7 = f32[2,64,64]{2,1,0:T(8,128)S(1)} custom-call(f32[2,64,64]{2,1,0:T(8,128)S(1)} %fusion.2), custom_call_target="Cholesky" | custom-call | tf_op jit(solution)/shard_map/jit(cholesky)/cholesky | solution.py:53
  213.4 0.1 compare_reduce_fusion
  213.5 0.1 select_bitcast_fusion
  213.6 9.8 %custom-call.8 = f32[2,1,64,64]{2,3,1,0:T(8,128)S(1)} custom-call(f32[2,1,64,64]{3,2,1,0:T(8,128)S(1)} %select_bitcast_fusion), custom_call_target="InvertDiagBlocksLowerTriangular" | custom-call | tf_op jit(solution)/shard_map/triangular_solve | solution.py:54
  223.4 2.0 fusion
  (11 shorter events, 0.2 us)
Async XLA Ops:
  7.2 151.9 %all-gather.2.cloned.1.call-start = ((), (), s32[]{:S(2)}) async-start(), calls=%async_computation | async-start | bytes 9437184 | tf_op jit(solution)/shard_map/all_gather | solution.py:43
  9.4 19.9 %copy-start = (bf16[512,16384]{1,0:T(8,128)(2,1)S(1)}, bf16[512,16384]{1,0:T(8,128)(2,1)}, u32[]{:S(2)}) copy-start(bf16[512,16384]{1,0:T(8,128)(2,1)} %param.2) | copy-start | bytes 50331652
  17.7 11.7 %collective-permute-start = (f32[4,1,16384]{2,0,1:T(4,128)S(1)}, f32[4,1,16384]{2,0,1:T(4,128)S(1)}, u32[]{:S(2)}, u32[]{:S(2)}) collective-permute-start(f32[4,1,16384]{2,0,1:T(4,128)S(1)} %slice.29), channel_id=1, source_target_pairs={{0,7},{1,0},{2,1},{3,2},{4,3},{5,4},{6,5},{7,6},{8,15},{9,8},{10,9... | collective-permute-start | bytes 786440 | tf_op jit(solution)/shard_map/ppermute | solution.py:14
Sparse Core Ops, SparseCore 0:
  32.7 126.3 all-gather.1
where the time goes:
time: 233 us; the launch traced here: 232 us
  waiting for transfers between devices  132 us (57%)
  blocking collectives  38.7 us (17%)
  other arithmetic  23.3 us (10%)
  between operations  14.8 us (6%)
  matrix products  14.6 us (6%)
  starting transfers between devices  6.12 us (3%)
  local copies, waits for them, and re-layouts  2.87 us (1%)
    all_gather x1, waiting for transfers between devices, on_device(): lax.all_gather(coeffs, 'tm', axis=1, tiled=True)  126 us
    psum x1, blocking collectives, on_device(): gram_matrix = lax.psum(partial_value, ('space', 'tm'))  38.7 us
    another operation x4, other arithmetic, on_device(): factor = jnp.linalg.cholesky(gram_matrix + ridge_term * identity[None])  11.9 us
    another operation x3, other arithmetic, on_device(): lax.linalg.triangular_solve(factor, columns, left_side=True, lower=True)  9.92 us
    dot_general x1, matrix products, on_device(): jnp.einsum('ct,htp->chp', second_table, halves, preferred_element_type=jn...  8.19 us
    ppermute x1, starting transfers between devices, passed_along(): lax.ppermute(array, axis, [(i, (i + by) % devices) for i in range(devices)])  6.09 us
    ppermute x1, waiting for transfers between devices, passed_along(): lax.ppermute(array, axis, [(i, (i + by) % devices) for i in range(devices)])  5.51 us
  transfers between devices with their start and end apart: 2, of which 2 were waited for; matrix products, arithmetic and copies ran while one was open for 0% of the time, Pallas kernels for 0%

commit v1 on v0

--- a/solution.py
+++ b/solution.py
@@ -1,3 +1,4 @@
+import functools
 import jax
 import jax.numpy as jnp
 from jax import lax
@@ -7,6 +8,15 @@
 HOP = 128
 NF = 2
 ridge_term = 0.01
+
+
+def render_ends(point, dev_axis):
+    work_now = jax.lax.all_gather(point, dev_axis)
+    kept_arr = jnp.sum(work_now, axis=0)
+    return kept_arr
+
+
+_part_field = functools.partial(render_ends, dev_axis=("space", "tm"))
 
 
 def passed_along(array, axis, by):
@@ -48,7 +58,7 @@
     partial_value = (
         jnp.einsum("fcp,fdp->fcd", columns, columns, precision=lax.Precision.HIGHEST) / grid_total
     )
-    gram_matrix = lax.psum(partial_value, ("space", "tm"))
+    gram_matrix = _part_field(partial_value)
     identity = jnp.eye(2 * all_blocks_count, dtype=jnp.float32)
     factor = jnp.linalg.cholesky(gram_matrix + ridge_term * identity[None])
     whitened = lax.linalg.triangular_solve(factor, columns, left_side=True, lower=True)

time: 233 us -> 250 us (1.073)
  waiting for transfers between devices: 132 us -> 187 us
  blocking collectives: 38.7 us -> 0 us
    all_gather x0 -> x1, waiting for transfers between devices: none -> 54.6 us  [render_ends(): work_now = jax.lax.all_gather(point, dev_axis)]
    psum x1 -> x0, blocking collectives: 38.7 us -> none  [on_device(): gram_matrix = lax.psum(partial_value, ('space', 'tm'))]
  transfers between devices with their start and end apart: 2 -> 3, of which waited for: 2 -> 3; matrix products, arithmetic and copies ran while one was open for 0% -> 0% of each run, Pallas kernels for 0% -> 0%
where the time goes in v1:
time: 250 us
  waiting for transfers between devices  187 us (75%)
  other arithmetic  25.1 us (10%)
  matrix products  15.2 us (6%)
  between operations  14.8 us (6%)
  starting transfers between devices  6.16 us (2%)
    all_gather x1, waiting for transfers between devices, on_device(): lax.all_gather(coeffs, 'tm', axis=1, tiled=True)  126 us
    all_gather x1, waiting for transfers between devices, render_ends(): work_now = jax.lax.all_gather(point, dev_axis)  54.6 us
    another operation x4, other arithmetic, on_device(): factor = jnp.linalg.cholesky(gram_matrix + ridge_term * identity[None])  11.9 us
    another operation x3, other arithmetic, on_device(): lax.linalg.triangular_solve(factor, columns, left_side=True, lower=True)  9.92 us
    dot_general x1, matrix products, on_device(): jnp.einsum('ct,htp->chp', second_table, halves, preferred_element_type=jn...  8.19 us
    ppermute x1, starting transfers between devices, passed_along(): lax.ppermute(array, axis, [(i, (i + by) % devices) for i in range(devices)])  6.09 us
    ppermute x1, waiting for transfers between devices, passed_along(): lax.ppermute(array, axis, [(i, (i + by) % devices) for i in range(devices)])  5.51 us
  transfers between devices with their start and end apart: 3, of which 3 were waited for; matrix products, arithmetic and copies ran while one was open for 0% of the time, Pallas kernels for 0%

profile of v1, /device:TPU:0, one launch (start us, length us, event | category | flops | bytes accessed | tf_op | source)
XLA Modules:
  0.0 250.0 jit_solution(6272371269823234661)
XLA Ops:
  7.2 0.0 all-gather.4.cloned.1.call-start
  7.2 0.6 multiply_reduce_fusion
  8.6 0.8 multiply_convert_fusion.1
  9.4 0.0 copy-start
  9.4 8.2 %fusion.8 = f32[4,4,16384]{2,0,1:T(4,128)S(1)} fusion(bf16[4,128,16384]{2,1,0:T(8,128)(2,1)} %bitcast.27, bf16[4,256]{1,0:T(4,128)(2,1)S(1)} %convert_element_type.35), kind=kOutput, calls=%fused_computation.25 | convolution fusion | flops 67108864 | bytes 17826816 | tf_op jit(solution)/shard_map/ct,htp->chp/dot_general | solution.py:46
  17.7 6.1 %collective-permute-start = (f32[4,1,16384]{2,0,1:T(4,128)S(1)}, f32[4,1,16384]{2,0,1:T(4,128)S(1)}, u32[]{:S(2)}, u32[]{:S(2)}) collective-permute-start(f32[4,1,16384]{2,0,1:T(4,128)S(1)} %slice.29), channel_id=1, source_target_pairs={{0,7},{1,0},{2,1},{3,2},{4,3},{5,4},{6,5},{7,6},{8,15},{9,8},{10,9... | collective-permute-start | bytes 786440 | tf_op jit(solution)/shard_map/ppermute | solution.py:24
  23.7 0.1 slice.28
  23.8 5.5 %collective-permute-done = f32[4,1,16384]{2,0,1:T(4,128)S(1)} collective-permute-done((f32[4,1,16384]{2,0,1:T(4,128)S(1)}, f32[4,1,16384]{2,0,1:T(4,128)S(1)}, u32[]{:S(2)}, u32[]{:S(2)}) %collective-permute-start) | collective-permute-done | bytes 262176 | tf_op jit(solution)/shard_map/ppermute | solution.py:24
  29.3 3.3 %maximum_add_fusion = f32[4,4,16384]{2,0,1:T(4,128)} fusion(f32[4,1,16384]{2,0,1:T(4,128)S(1)} %collective-permute-done, f32[4,3,16384]{2,0,1:T(4,128)S(1)} %slice.28, bf16[4,128,16384]{2,1,0:T(8,128)(2,1)S(1)} %bitcast.28, bf16[4,256]{1,0:T(4,128)(2,1)S(1)} %convert_element_type.35), kind=kOutput, calls=%fused_computation.1 | convolution fusion | flops 67633152 | bytes 18875392 | tf_op jit(solution)/shard_map/ct,htp->chp/dot_general | solution.py:45
  32.6 0.0 all-gather.4.cloned.1.call-update
  32.6 0.0 all-gather.6.cloned.1.call-start
  32.6 126.4 %all-gather.4.cloned.1.call-done = f32[4,32,16384]{2,0,1:T(4,128)} async-done(((f32[4,4,16384]{2,0,1:T(4,128)}), f32[4,32,16384]{2,0,1:T(4,128)}) %all-gather.4.cloned.1.call-update) | async-done | bytes 8388624 | tf_op jit(solution)/shard_map/all_gather | solution.py:53
  159.1 1.3 constant_dynamic-slice_fusion
  160.4 0.6 copy.27
  161.0 1.7 convolution_multiply_fusion
  162.7 0.0 all-gather.6.cloned.1.call-update
  162.8 54.6 %all-gather.6.cloned.1.call-done = f32[64,64,64]{2,1,0:T(8,128)} async-done(((f32[2,64,64]{2,1,0:T(8,128)}), f32[64,64,64]{2,1,0:T(8,128)}) %all-gather.6.cloned.1.call-update) | async-done | bytes 1048592 | tf_op jit(solution)/shard_map/all_gather | solution.py:14
  217.5 1.8 reduce_sum.21
  219.2 0.1 copy.24
  219.3 11.7 %custom-call.7 = f32[2,64,64]{2,1,0:T(8,128)S(1)} custom-call(f32[2,64,64]{2,1,0:T(8,128)S(1)} %fusion.3), custom_call_target="Cholesky" | custom-call | tf_op jit(solution)/shard_map/jit(cholesky)/cholesky | solution.py:63
  231.1 0.1 compare_reduce_fusion
  231.2 0.1 select_bitcast_fusion
  231.3 9.8 %custom-call.8 = f32[2,1,64,64]{2,3,1,0:T(8,128)S(1)} custom-call(f32[2,1,64,64]{3,2,1,0:T(8,128)S(1)} %select_bitcast_fusion), custom_call_target="InvertDiagBlocksLowerTriangular" | custom-call | tf_op jit(solution)/shard_map/triangular_solve | solution.py:64
  241.1 2.0 fusion
  (13 shorter events, 0.2 us)
Async XLA Ops:
  7.2 151.9 %all-gather.4.cloned.1.call-start = ((), (), s32[]{:S(2)}) async-start(), calls=%async_computation | async-start | bytes 9437184 | tf_op jit(solution)/shard_map/all_gather | solution.py:53
  9.4 19.9 %copy-start = (bf16[512,16384]{1,0:T(8,128)(2,1)S(1)}, bf16[512,16384]{1,0:T(8,128)(2,1)}, u32[]{:S(2)}) copy-start(bf16[512,16384]{1,0:T(8,128)(2,1)} %param.2) | copy-start | bytes 50331652
  17.7 11.7 %collective-permute-start = (f32[4,1,16384]{2,0,1:T(4,128)S(1)}, f32[4,1,16384]{2,0,1:T(4,128)S(1)}, u32[]{:S(2)}, u32[]{:S(2)}) collective-permute-start(f32[4,1,16384]{2,0,1:T(4,128)S(1)} %slice.29), channel_id=1, source_target_pairs={{0,7},{1,0},{2,1},{3,2},{4,3},{5,4},{6,5},{7,6},{8,15},{9,8},{10,9... | collective-permute-start | bytes 786440 | tf_op jit(solution)/shard_map/ppermute | solution.py:24
  32.6 184.9 %all-gather.6.cloned.1.call-start = ((), (), s32[]{:S(2)}) async-start(), calls=%async_computation.1 | async-start | bytes 2162688 | tf_op jit(solution)/shard_map/all_gather | solution.py:14
  219.2 23.9 %copy-start.1 = (f32[2,64,64]{2,1,0:T(8,128)}, f32[2,64,64]{2,1,0:T(8,128)S(1)}, u32[]{:S(2)}) copy-start(f32[2,64,64]{2,1,0:T(8,128)S(1)} %reduce_sum.21) | copy-start | bytes 98308
Sparse Core Ops, SparseCore 0:
  32.7 126.3 all-gather.3
  162.9 54.5 all-gather.5
